TPU v7x, 256 devices: a whole 4x4x8 slice. The times are simulated.
256 devices in a mesh: group: 2 (over z_lo), dp: 16 (over y, z_hi), mp: 8 (over x, core).
Axes of the slice: x: 4, y: 4, z: 8 (z_hi: 4, z_lo: 2; z = z_hi * 2 + z_lo), core: 2. Of those that a mesh axis runs over, the one named last changes fastest.
Arguments:
- teacher_hidden: bfloat16 [2048, 8192], P('dp', ('group', 'mp')), may hold values from -6 to 6
- teacher_gain: bfloat16 [8192], P(('group', 'mp')), may hold values from 0.25 to 1.75
- teacher_head: bfloat16 [8192, 8192], P(('group', 'mp')), may hold values from -0.198873782 to 0.198873782
- student_hidden: bfloat16 [2048, 4096], P('dp'), may hold values from -6 to 6
- student_head: bfloat16 [4096, 8192], P('dp', ('group', 'mp')), may hold values from -0.28125 to 0.28125
- depth_cut: int32 [32], P('dp'), may hold values from 1 to 4
Outputs:
- kl_terms: float32 [4, 2048], P(None, 'dp')
- hidden_grad: float32 [2048, 4096], P('dp', ('group', 'mp'))
- head_grad: float32 [4096, 8192], P('dp', ('group', 'mp'))
Inputs may be any that keep to these rules, and one draw needn't show every extreme that they name: `depth_cut`: each sample's number of codebooks kept.
All inputs are finite; a program needn't handle non-finite values.
Results may differ from a plain program's by a relative error of at most 0.0053.
Values may be sent and summed in bfloat16 or wider, within the bound.
No kernel may reach another device: no remote copies, remote signals or barrier semaphores. Data moves between devices by JAX's collectives and lax.ppermute only.
A program may use at most 128 MiB of HBM per device.

v0:
```python
import jax
import jax.numpy as jnp
from jax import lax
from jax.sharding import PartitionSpec as P

DT = 8192
C = 4
V = 2048
FRAMES = 64
epsilon = 1e-05


def from_everyone(value, axis):
    size = lax.axis_size(axis)
    return lax.all_to_all(
        jnp.broadcast_to(value[None], (size, *value.shape)), axis, 0, 0, tiled=True
    )


def of_everyone(value, axis):
    return from_everyone(value, axis).sum(axis=0)


def laid_out(parts, dim):
    parts = jnp.moveaxis(parts, 0, dim)
    shape = parts.shape
    return parts.reshape(*shape[:dim], shape[dim] * shape[dim + 1], *shape[dim + 2 :])


def gather_directly(value, axis, dim):
    return laid_out(from_everyone(value, axis), dim)


def in_blocks(value, dim, size):
    before, after = (value.shape[:dim], value.shape[dim + 1 :])
    return jnp.moveaxis(value.reshape(*before, size, -1, *after), dim, 0)


def sent_and_summed(value, axis, dim):
    size = lax.axis_size(axis)
    parts = lax.all_to_all(in_blocks(value, dim, size), axis, 0, 0, tiled=True)
    return jnp.sum(parts, axis=0)


def shards(teacher_hidden, teacher_gain, teacher_head, student_hidden, student_head, depth_cut):
    part_count = lax.axis_size(("group", "mp"))
    device_index = lax.axis_index(("group", "mp"))
    frame_count = teacher_hidden.shape[0]
    hidden_float = teacher_hidden.astype(jnp.float32)
    squares = of_everyone(jnp.sum(hidden_float * hidden_float, axis=1), ("group", "mp"))
    row_scale = lax.rsqrt(squares / DT + epsilon)
    normed = (hidden_float * row_scale[:, None] * teacher_gain.astype(jnp.float32)[None, :]).astype(
        jnp.bfloat16
    )
    student_full = lax.all_gather(student_head, "dp", axis=0, tiled=True)
    depth_rows = jnp.repeat(depth_cut, FRAMES)
    book_range = jnp.arange(C, dtype=jnp.int32)
    alive_mask = (book_range[None, :] < depth_rows[:, None]).astype(jnp.float32)
    depth_weight = alive_mask / depth_rows[:, None].astype(jnp.float32)
    row_total = frame_count // part_count
    sliced = normed
    teacher_rows = lax.psum_scatter(
        jnp.dot(sliced, teacher_head, preferred_element_type=jnp.float32),
        ("group", "mp"),
        scatter_dimension=0,
        tiled=True,
    )
    student_part = jnp.dot(student_hidden, student_full, preferred_element_type=jnp.float32)
    student_rows = lax.all_to_all(
        student_part, ("group", "mp"), split_axis=0, concat_axis=1, tiled=True
    )
    teacher_log = jax.nn.log_softmax(teacher_rows.reshape(row_total, C, V), axis=2)
    student_log = jax.nn.log_softmax(student_rows.reshape(row_total, C, V), axis=2)
    teacher_prob = jnp.exp(teacher_log)
    divergence = jnp.sum(teacher_prob * (teacher_log - student_log), axis=2)
    weight_rows = lax.dynamic_slice_in_dim(depth_weight, device_index * row_total, row_total, 0)
    kl_terms = gather_directly((divergence * weight_rows).T, ("group", "mp"), 1)
    grad_rows = (
        ((jnp.exp(student_log) - teacher_prob) * weight_rows[:, :, None])
        .reshape(row_total, C * V)
        .astype(jnp.bfloat16)
    )
    score_grad = lax.all_to_all(grad_rows, ("group", "mp"), split_axis=1, concat_axis=0, tiled=True)
    hidden_term = lax.dot_general(
        score_grad, student_full, (((1,), (1,)), ((), ())), preferred_element_type=jnp.float32
    )
    head_dims = (((0,), (0,)), ((), ()))
    hidden_grad = sent_and_summed(hidden_term, ("group", "mp"), 1)
    sliced = student_hidden
    head_grad = lax.psum_scatter(
        lax.dot_general(sliced, score_grad, head_dims, preferred_element_type=jnp.float32),
        "dp",
        scatter_dimension=0,
        tiled=True,
    )
    return (kl_terms, hidden_grad, head_grad)


def solution(mesh):
    return jax.shard_map(
        shards,
        mesh=mesh,
        in_specs=(
            P("dp", ("group", "mp")),
            P(("group", "mp")),
            P(("group", "mp"), None),
            P("dp", None),
            P("dp", ("group", "mp")),
            P("dp"),
        ),
        out_specs=(P(None, "dp"), P("dp", ("group", "mp")), P("dp", ("group", "mp"))),
        check_vma=False,
    )
```

profile of v0, /device:TPU:2, one launch (start us, length us, event | category | flops | bytes accessed | tf_op | source)
XLA Modules:
  0.0 294.2 jit_solution(6305861253287781479)
XLA Ops:
  8.1 0.7 all-gather.2.cloned.1.call-update
  8.7 1.0 fusion.10
  9.8 0.6 broadcast_in_dim.6
  10.4 6.2 %all-to-all-start = ((f32[16,1,128]{2,1,0:T(1,128)}), f32[16,1,128]{2,1,0:T(1,128)S(1)}, u32[]{:S(2)}, u32[]{:S(2)}) async-start(f32[16,1,128]{2,1,0:T(1,128)} %broadcast_in_dim.6), calls=%async_computation | async-start | bytes 16384 | tf_op jit(solution)/shard_map/all_to_all | solution.py:15
  16.6 0.0 reduce-scatter.3.cloned.1.call-start
  16.6 0.7 convert_element_type.28
  17.3 3.9 %all-to-all-done = f32[16,1,128]{2,1,0:T(1,128)S(1)} async-done(((f32[16,1,128]{2,1,0:T(1,128)}), f32[16,1,128]{2,1,0:T(1,128)S(1)}, u32[]{:S(2)}, u32[]{:S(2)}) %all-to-all-start) | async-done | bytes 8224 | tf_op jit(solution)/shard_map/all_to_all | solution.py:15
  21.2 6.7 %fusion.15 = f32[128,8192]{1,0:T(8,128)} fusion(bf16[512,8192]{1,0:T(8,128)(2,1)} %param.9, bf16[128,512]{1,0:T(8,128)(2,1)} %param.7, f32[512]{0:T(512)S(1)} %convert_element_type.28, f32[128]{0:T(128)S(1)} %add_rsqrt_fusion), kind=kOutput, calls=%fused_computation.24 | convolution fusion | flops 1074003968 | bytes 12716544 | tf_op jit(solution)/shard_map/dot_general | solution.py:63
  28.0 61.3 %all-gather.2.cloned.1.call-done = bf16[4096,512]{1,0:T(8,128)(2,1)} async-done(((bf16[256,512]{1,0:T(8,128)(2,1)}), bf16[4096,512]{1,0:T(8,128)(2,1)}) %all-gather.2.cloned.1.call-update) | async-done | bytes 4194320 | tf_op jit(solution)/shard_map/all_gather | solution.py:55
  89.3 3.6 %convolution_bitcast_fusion.2 = f32[16,8,512]{2,1,0:T(8,128)} fusion(bf16[128,4096]{1,0:T(8,128)(2,1)S(1)} %copy-done, bf16[4096,512]{1,0:T(8,128)(2,1)} %all-gather.2.cloned.1.call-done), kind=kOutput, calls=%fused_computation.12 | convolution fusion | flops 536870912 | bytes 5505024 | tf_op jit(solution)/shard_map/dot_general | solution.py:68
  93.0 11.4 %all-to-all-start.1 = ((f32[16,8,512]{2,1,0:T(8,128)}), f32[16,8,512]{2,1,0:T(8,128)S(1)}, u32[]{:S(2)}, u32[]{:S(2)}) async-start(f32[16,8,512]{2,1,0:T(8,128)} %convolution_bitcast_fusion.2), calls=%async_computation.2 | async-start | bytes 524288 | tf_op jit(solution)/shard_map/all_to_all | solution.py:69
  104.4 0.1 broadcast_in_dim.7
  104.5 0.1 lt.19
  104.6 5.7 %all-to-all-done.1 = f32[16,8,512]{2,1,0:T(8,128)S(1)} async-done(((f32[16,8,512]{2,1,0:T(8,128)}), f32[16,8,512]{2,1,0:T(8,128)S(1)}, u32[]{:S(2)}, u32[]{:S(2)}) %all-to-all-start.1) | async-done | bytes 262176 | tf_op jit(solution)/shard_map/all_to_all | solution.py:69
  110.3 0.4 fusion.5
  110.7 0.4 fusion.8
  111.1 15.1 %reduce-scatter.3.cloned.1.call-done = f32[8,8192]{1,0:T(8,128)} async-done(((f32[128,8192]{1,0:T(8,128)}), f32[8,8192]{1,0:T(8,128)}) %reduce-scatter.3.cloned.1.call-update) | async-done | bytes 262160 | tf_op jit(solution)/shard_map/reduce_scatter | solution.py:62
  126.2 1.1 fusion.4
  127.3 0.9 multiply_reduce_fusion
  128.2 0.1 multiply_bitcast_fusion
  128.3 0.1 multiply_convert_fusion
  128.4 12.0 %all_to_all.48 = bf16[8,16,512]{2,0,1:T(8,128)(2,1)S(1)} all-to-all(bf16[8,16,512]{2,0,1:T(8,128)(2,1)S(1)} %bitcast.34), channel_id=1, replica_groups=mesh['group'=2,'dp'=16,'mp'=8] {'group','mp'}, dimensions={1} | all-to-all | bytes 262144 | tf_op jit(solution)/shard_map/all_to_all | solution.py:83
  140.4 4.5 %convolution_bitcast_fusion = f32[4096,512]{0,1:T(8,128)} fusion(bf16[128,4096]{1,0:T(8,128)(2,1)S(1)} %copy-done, bf16[8,16,512]{2,0,1:T(8,128)(2,1)S(1)} %all_to_all.48), kind=kOutput, calls=%fused_computation.4 | convolution fusion | flops 536870912 | bytes 9568256 | tf_op jit(solution)/shard_map/dot_general | solution.py:91
  144.9 0.6 broadcast_in_dim.8
  145.5 5.2 %all-to-all-start.2 = ((f32[16,4,8]{2,1,0:T(4,128)}), f32[16,4,8]{2,1,0:T(4,128)S(1)}, u32[]{:S(2)}, u32[]{:S(2)}) async-start(f32[16,4,8]{2,1,0:T(4,128)} %broadcast_in_dim.8), calls=%async_computation.3 | async-start | bytes 65536 | tf_op jit(solution)/shard_map/all_to_all | solution.py:15
  150.7 5.0 %convolution_bitcast_fusion.1 = f32[16,128,256]{2,1,0:T(8,128)} fusion(bf16[16,256,512]{2,1,0:T(8,128)(2,1)} %bitcast.32, bf16[8,16,512]{2,0,1:T(8,128)(2,1)S(1)} %all_to_all.48), kind=kOutput, calls=%fused_computation.11 | convolution fusion | flops 536870912 | bytes 6422528 | tf_op jit(solution)/shard_map/dot_general | solution.py:84
  155.7 5.8 %all-to-all-start.4 = ((f32[16,128,256]{2,1,0:T(8,128)}), f32[16,128,256]{2,1,0:T(8,128)S(1)}, u32[]{:S(2)}, u32[]{:S(2)}) async-start(f32[16,128,256]{2,1,0:T(8,128)} %convolution_bitcast_fusion.1), calls=%async_computation.5 | async-start | bytes 4194304 | tf_op jit(solution)/shard_map/all_to_all | solution.py:41
  161.5 0.7 reshape.56
  162.2 67.3 %all-to-all-done.4 = f32[16,128,256]{2,1,0:T(8,128)S(1)} async-done(((f32[16,128,256]{2,1,0:T(8,128)}), f32[16,128,256]{2,1,0:T(8,128)S(1)}, u32[]{:S(2)}, u32[]{:S(2)}) %all-to-all-start.4) | async-done | bytes 2097184 | tf_op jit(solution)/shard_map/all_to_all | solution.py:41
  229.5 0.8 reduce_sum.48
  230.3 54.4 %reduce-scatter.5.cloned.1.call-done = f32[256,512]{0,1:T(8,128)} async-done(((f32[4096,512]{0,1:T(8,128)}), f32[256,512]{0,1:T(8,128)}) %reduce-scatter.5.cloned.1.call-update) | async-done | bytes 524304 | tf_op jit(solution)/shard_map/reduce_scatter | solution.py:90
  284.7 2.0 copy.17
  (14 shorter events, 0.2 us)
Async XLA Ops:
  8.0 81.3 %copy-start = (bf16[128,4096]{1,0:T(8,128)(2,1)S(1)}, bf16[128,4096]{1,0:T(8,128)(2,1)}, u32[]{:S(2)}) copy-start(bf16[128,4096]{1,0:T(8,128)(2,1)} %param.10) | copy-start | bytes 3145732
  8.0 81.3 %all-gather.2.cloned.1.call-start = ((), (), s32[]{:S(2)}) async-start(), calls=%async_computation.8 | async-start | bytes 4456448 | tf_op jit(solution)/shard_map/all_gather | solution.py:55
  10.4 10.8 %all-to-all-start = ((f32[16,1,128]{2,1,0:T(1,128)}), f32[16,1,128]{2,1,0:T(1,128)S(1)}, u32[]{:S(2)}, u32[]{:S(2)}) async-start(f32[16,1,128]{2,1,0:T(1,128)} %broadcast_in_dim.6), calls=%async_computation | async-start | bytes 16384 | tf_op jit(solution)/shard_map/all_to_all | solution.py:15
  16.6 109.6 %reduce-scatter.3.cloned.1.call-start = ((), (), s32[]{:S(2)}) async-start(), calls=%async_computation.7 | async-start | bytes 4456448 | tf_op jit(solution)/shard_map/reduce_scatter | solution.py:62
  27.9 76.5 %copy-start.1 = (s32[2]{0:T(128)S(1)}, s32[2]{0:T(128)}, u32[]{:S(2)}) copy-start(s32[2]{0:T(128)} %param.12) | copy-start | bytes 28
  93.0 17.4 %all-to-all-start.1 = ((f32[16,8,512]{2,1,0:T(8,128)}), f32[16,8,512]{2,1,0:T(8,128)S(1)}, u32[]{:S(2)}, u32[]{:S(2)}) async-start(f32[16,8,512]{2,1,0:T(8,128)} %convolution_bitcast_fusion.2), calls=%async_computation.2 | async-start | bytes 524288 | tf_op jit(solution)/shard_map/all_to_all | solution.py:69
  104.4 180.3 %reduce-scatter.5.cloned.1.call-start = ((), (), s32[]{:S(2)}) async-start(), calls=%async_computation.9 | async-start | bytes 8912896 | tf_op jit(solution)/shard_map/reduce_scatter | solution.py:90
  145.5 10.2 %all-to-all-start.2 = ((f32[16,4,8]{2,1,0:T(4,128)}), f32[16,4,8]{2,1,0:T(4,128)S(1)}, u32[]{:S(2)}, u32[]{:S(2)}) async-start(f32[16,4,8]{2,1,0:T(4,128)} %broadcast_in_dim.8), calls=%async_computation.3 | async-start | bytes 65536 | tf_op jit(solution)/shard_map/all_to_all | solution.py:15
  155.7 73.8 %all-to-all-start.4 = ((f32[16,128,256]{2,1,0:T(8,128)}), f32[16,128,256]{2,1,0:T(8,128)S(1)}, u32[]{:S(2)}, u32[]{:S(2)}) async-start(f32[16,128,256]{2,1,0:T(8,128)} %convolution_bitcast_fusion.1), calls=%async_computation.5 | async-start | bytes 4194304 | tf_op jit(solution)/shard_map/all_to_all | solution.py:41
Sparse Core Ops, SparseCore 0:
  11.3 78.0 all-gather.1
  145.0 139.6 reduce-scatter.4
Sparse Core Ops, SparseCore 1:
  28.1 98.1 reduce-scatter.2
where the time goes:
time: 295 us; the launch traced here: 294 us
  waiting for transfers between devices  208 us (71%)
  starting transfers between devices  28.7 us (10%)
  matrix products  19.9 us (7%)
  between operations  15.5 us (5%)
  blocking collectives  12 us (4%)
  other arithmetic  5.51 us (2%)
  local copies, waits for them, and re-layouts  4.11 us (1%)
    all_to_all x1, waiting for transfers between devices, sent_and_summed(): parts = lax.all_to_all(in_blocks(value, dim, size), axis, 0, 0, tiled=True)  67.3 us
    all_gather x1, waiting for transfers between devices, shards(): student_full = lax.all_gather(student_head, 'dp', axis=0, tiled=True)  61.3 us
    reduce_scatter x1, waiting for transfers between devices, shards(): lax.psum_scatter(lax.dot_general(sliced, score_grad, head_dims, preferred...  54.4 us
    reduce_scatter x1, waiting for transfers between devices, shards(): lax.psum_scatter(jnp.dot(sliced, teacher_head, preferred_element_type=jnp...  15.1 us
    all_to_all x1, blocking collectives, shards(): lax.all_to_all(grad_rows, ('group', 'mp'), split_axis=1, concat_axis=0, t...  12 us
    all_to_all x1, starting transfers between devices, shards(): lax.all_to_all(student_part, ('group', 'mp'), split_axis=0, concat_axis=1...  11.4 us
    all_to_all x2, starting transfers between devices, from_everyone(): lax.all_to_all(jnp.broadcast_to(value[None], (size, *value.shape)), axis,...  11.4 us
    dot_general x1, matrix products, shards(): jnp.dot(sliced, teacher_head, preferred_element_type=jnp.float32)  6.7 us
  transfers between devices with their start and end apart: 7, of which 6 were waited for; matrix products, arithmetic and copies ran while one was open for 7% of the time, Pallas kernels for 0%

commit v1 on v0

--- a/solution.py
+++ b/solution.py
@@ -52,7 +52,9 @@
     normed = (hidden_float * row_scale[:, None] * teacher_gain.astype(jnp.float32)[None, :]).astype(
         jnp.bfloat16
     )
-    student_full = lax.all_gather(student_head, "dp", axis=0, tiled=True)
+    student_full = jnp.concatenate(
+        lax.all_to_all(jnp.stack([student_head] * lax.axis_size("dp")), "dp", 0, 0), axis=0
+    )
     depth_rows = jnp.repeat(depth_cut, FRAMES)
     book_range = jnp.arange(C, dtype=jnp.int32)
     alive_mask = (book_range[None, :] < depth_rows[:, None]).astype(jnp.float32)

time: 295 us -> 323 us (1.095)
  waiting for transfers between devices: 208 us -> 219 us
  blocking collectives: 12 us -> 20.8 us
  starting transfers between devices: 28.7 us -> 36.5 us
    all_to_all x0 -> x1, waiting for transfers between devices: none -> 96.3 us  [shards(): lax.all_to_all(jnp.stack([student_head] * lax.axis_size('dp')), 'dp', 0, 0)]
    all_gather x1 -> x0, waiting for transfers between devices: 61.3 us -> none  [shards(): student_full = lax.all_gather(student_head, 'dp', axis=0, tiled=True)]
    reduce_scatter x1, waiting for transfers between devices: 15.1 us -> 0.01 us  [shards(): lax.psum_scatter(jnp.dot(sliced, teacher_head, preferred_element_type=jnp...]
    all_to_all x0 -> x1, blocking collectives: none -> 10.7 us  [from_everyone(): lax.all_to_all(jnp.broadcast_to(value[None], (size, *value.shape)), axis,...]
    all_to_all x0 -> x1, starting transfers between devices: none -> 10.5 us  [shards(): lax.all_to_all(jnp.stack([student_head] * lax.axis_size('dp')), 'dp', 0, 0)]
    all_to_all x2 -> x1, starting transfers between devices: 11.4 us -> 5.19 us  [from_everyone(): lax.all_to_all(jnp.broadcast_to(value[None], (size, *value.shape)), axis,...]
    reduce_scatter x1, waiting for transfers between devices: 54.4 us -> 50 us  [shards(): lax.psum_scatter(lax.dot_general(sliced, score_grad, head_dims, preferred...]
    all_to_all x2 -> x1, waiting for transfers between devices: 3.91 us -> 0.01 us  [from_everyone(): lax.all_to_all(jnp.broadcast_to(value[None], (size, *value.shape)), axis,...]
  transfers between devices with their start and end apart: 7 -> 6, of which waited for: 6 -> 4; matrix products, arithmetic and copies ran while one was open for 7% -> 6% of each run, Pallas kernels for 0% -> 0%
where the time goes in v1:
time: 323 us; the launch traced here: 322 us
  waiting for transfers between devices  219 us (68%)
  starting transfers between devices  36.5 us (11%)
  blocking collectives  20.8 us (6%)
  matrix products  20.2 us (6%)
  between operations  14.1 us (4%)
  local copies, waits for them, and re-layouts  6.79 us (2%)
  other arithmetic  4.93 us (2%)
    all_to_all x1, waiting for transfers between devices, shards(): lax.all_to_all(jnp.stack([student_head] * lax.axis_size('dp')), 'dp', 0, 0)  96.3 us
    all_to_all x1, waiting for transfers between devices, sent_and_summed(): parts = lax.all_to_all(in_blocks(value, dim, size), axis, 0, 0, tiled=True)  67.5 us
    reduce_scatter x1, waiting for transfers between devices, shards(): lax.psum_scatter(lax.dot_general(sliced, score_grad, head_dims, preferred...  50 us
    all_to_all x1, starting transfers between devices, shards(): lax.all_to_all(student_part, ('group', 'mp'), split_axis=0, concat_axis=1...  14.9 us
    all_to_all x1, blocking collectives, from_everyone(): lax.all_to_all(jnp.broadcast_to(value[None], (size, *value.shape)), axis,...  10.7 us
    all_to_all x1, starting transfers between devices, shards(): lax.all_to_all(jnp.stack([student_head] * lax.axis_size('dp')), 'dp', 0, 0)  10.5 us
    all_to_all x1, blocking collectives, shards(): lax.all_to_all(grad_rows, ('group', 'mp'), split_axis=1, concat_axis=0, t...  10.1 us
    dot_general x1, matrix products, shards(): jnp.dot(sliced, teacher_head, preferred_element_type=jnp.float32)  6.67 us
  transfers between devices with their start and end apart: 6, of which 4 were waited for; matrix products, arithmetic and copies ran while one was open for 6% of the time, Pallas kernels for 0%

profile of v1, /device:TPU:2, one launch (start us, length us, event | category | flops | bytes accessed | tf_op | source)
XLA Modules:
  0.0 322.4 jit_solution(13203745470821882301)
XLA Ops:
  7.2 1.1 fusion.12
  8.3 10.7 %all_to_all.50 = f32[16,1,128]{2,1,0:T(1,128)S(1)} all-to-all(f32[16,1,128]{2,1,0:T(1,128)S(1)} %broadcast_in_dim.6), channel_id=1, replica_groups=mesh['group'=2,'dp'=16,'mp'=8] {'group','mp'}, dimensions={0} | all-to-all | bytes 16384 | tf_op jit(solution)/shard_map/all_to_all | solution.py:15
  19.0 3.3 %stack.2 = bf16[16,256,512]{2,1,0:T(8,128)(2,1)} broadcast(bf16[256,512]{1,0:T(8,128)(2,1)} %param.11), dimensions={1,2} | broadcast | bytes 4456448 | tf_op jit(solution)/shard_map/stack | solution.py:56
  22.3 10.5 %all-to-all-start.1 = ((bf16[16,256,512]{2,1,0:T(8,128)(2,1)}), bf16[16,256,512]{2,1,0:T(8,128)(2,1)}, u32[]{:S(2)}, u32[]{:S(2)}) async-start(bf16[16,256,512]{2,1,0:T(8,128)(2,1)} %stack.2), calls=%async_computation.2 | async-start | bytes 8388608 | tf_op jit(solution)/shard_map/all_to_all | solution.py:56
  32.8 0.0 reduce-scatter.3.cloned.1.call-start
  32.9 6.7 %fusion.17 = f32[128,8192]{1,0:T(8,128)} fusion(bf16[512,8192]{1,0:T(8,128)(2,1)} %param.9, bf16[128,512]{1,0:T(8,128)(2,1)S(1)} %copy-done.1, f32[512]{0:T(512)S(1)} %convert_element_type.28, f32[128]{0:T(128)S(1)} %add_rsqrt_fusion), kind=kOutput, calls=%fused_computation.25 | convolution fusion | flops 1074003968 | bytes 12716544 | tf_op jit(solution)/shard_map/dot_general | solution.py:65
  39.6 0.0 reduce-scatter.3.cloned.1.call-update
  39.6 96.3 %all-to-all-done.1 = bf16[16,256,512]{2,1,0:T(8,128)(2,1)} async-done(((bf16[16,256,512]{2,1,0:T(8,128)(2,1)}), bf16[16,256,512]{2,1,0:T(8,128)(2,1)}, u32[]{:S(2)}, u32[]{:S(2)}) %all-to-all-start.1) | async-done | bytes 4194336 | tf_op jit(solution)/shard_map/all_to_all | solution.py:56
  135.9 3.6 %fusion.10 = f32[16,8,512]{2,1,0:T(8,128)} fusion(bf16[4096,512,1]{1,0,2:T(8,128)(2,1)} %bitcast.4, bf16[128,4096]{1,0:T(8,128)(2,1)S(1)} %copy-done), kind=kOutput, calls=%fused_computation.12 | convolution fusion | flops 536870912 | bytes 5505024 | tf_op jit(solution)/shard_map/dot_general | solution.py:70
  139.5 14.9 %all-to-all-start.2 = ((f32[16,8,512]{2,1,0:T(8,128)}), f32[16,8,512]{2,1,0:T(8,128)S(1)}, u32[]{:S(2)}, u32[]{:S(2)}) async-start(f32[16,8,512]{2,1,0:T(8,128)} %fusion.10), calls=%async_computation.3 | async-start | bytes 524288 | tf_op jit(solution)/shard_map/all_to_all | solution.py:71
  154.5 0.0 reduce-scatter.5.cloned.1.call-start
  154.5 0.1 broadcast_in_dim.7
  154.6 0.1 lt.19
  154.7 5.2 %all-to-all-done.2 = f32[16,8,512]{2,1,0:T(8,128)S(1)} async-done(((f32[16,8,512]{2,1,0:T(8,128)}), f32[16,8,512]{2,1,0:T(8,128)S(1)}, u32[]{:S(2)}, u32[]{:S(2)}) %all-to-all-start.2) | async-done | bytes 262176 | tf_op jit(solution)/shard_map/all_to_all | solution.py:71
  159.9 0.4 fusion.5
  160.3 0.4 fusion.8
  160.8 1.1 fusion.4
  161.9 0.9 multiply_reduce_fusion
  162.8 0.1 multiply_bitcast_fusion
  162.8 0.1 multiply_convert_fusion
  163.0 10.1 %all_to_all.51 = bf16[8,16,512]{2,0,1:T(8,128)(2,1)S(1)} all-to-all(bf16[8,16,512]{2,0,1:T(8,128)(2,1)S(1)} %bitcast.35), channel_id=1, replica_groups=mesh['group'=2,'dp'=16,'mp'=8] {'group','mp'}, dimensions={1} | all-to-all | bytes 262144 | tf_op jit(solution)/shard_map/all_to_all | solution.py:85
  173.1 4.5 %convolution_bitcast_fusion = f32[4096,512]{0,1:T(8,128)} fusion(bf16[128,4096]{1,0:T(8,128)(2,1)S(1)} %copy-done, bf16[8,16,512]{2,0,1:T(8,128)(2,1)S(1)} %all_to_all.51), kind=kOutput, calls=%fused_computation.4 | convolution fusion | flops 536870912 | bytes 9568256 | tf_op jit(solution)/shard_map/dot_general | solution.py:93
  177.6 0.0 reduce-scatter.5.cloned.1.call-update
  177.6 0.6 broadcast_in_dim.8
  178.2 5.2 %all-to-all-start.3 = ((f32[16,4,8]{2,1,0:T(4,128)}), f32[16,4,8]{2,1,0:T(4,128)S(1)}, u32[]{:S(2)}, u32[]{:S(2)}) async-start(f32[16,4,8]{2,1,0:T(4,128)} %broadcast_in_dim.8), calls=%async_computation.4 | async-start | bytes 65536 | tf_op jit(solution)/shard_map/all_to_all | solution.py:15
  183.4 5.4 %convolution_bitcast_fusion.1 = f32[16,128,256]{2,1,0:T(8,128)} fusion(bf16[16,256,512]{2,1,0:T(8,128)(2,1)} %all-to-all-done.1, bf16[8,16,512]{2,0,1:T(8,128)(2,1)S(1)} %all_to_all.51), kind=kOutput, calls=%fused_computation.11 | convolution fusion | flops 536870912 | bytes 6422528 | tf_op jit(solution)/shard_map/dot_general | solution.py:86
  188.8 5.8 %all-to-all-start.5 = ((f32[16,128,256]{2,1,0:T(8,128)}), f32[16,128,256]{2,1,0:T(8,128)S(1)}, u32[]{:S(2)}, u32[]{:S(2)}) async-start(f32[16,128,256]{2,1,0:T(8,128)} %convolution_bitcast_fusion.1), calls=%async_computation.6 | async-start | bytes 4194304 | tf_op jit(solution)/shard_map/all_to_all | solution.py:41
  194.6 0.7 reshape.64
  195.3 67.5 %all-to-all-done.5 = f32[16,128,256]{2,1,0:T(8,128)S(1)} async-done(((f32[16,128,256]{2,1,0:T(8,128)}), f32[16,128,256]{2,1,0:T(8,128)S(1)}, u32[]{:S(2)}, u32[]{:S(2)}) %all-to-all-start.5) | async-done | bytes 2097184 | tf_op jit(solution)/shard_map/all_to_all | solution.py:41
  262.8 0.8 reduce_sum.48
  263.5 50.0 %reduce-scatter.5.cloned.1.call-done = f32[256,512]{0,1:T(8,128)} async-done(((f32[4096,512]{0,1:T(8,128)}), f32[256,512]{0,1:T(8,128)}) %reduce-scatter.5.cloned.1.call-update) | async-done | bytes 524304 | tf_op jit(solution)/shard_map/reduce_scatter | solution.py:92
  313.6 2.0 copy.17
  (17 shorter events, 0.1 us)
Async XLA Ops:
  7.2 128.7 %copy-start = (bf16[128,4096]{1,0:T(8,128)(2,1)S(1)}, bf16[128,4096]{1,0:T(8,128)(2,1)}, u32[]{:S(2)}) copy-start(bf16[128,4096]{1,0:T(8,128)(2,1)} %param.10) | copy-start | bytes 3145732
  22.3 10.5 %copy-start.2 = (bf16[512]{0:T(512)(128)(2,1)S(1)}, bf16[512]{0:T(512)(128)(2,1)}, u32[]{:S(2)}) copy-start(bf16[512]{0:T(512)(128)(2,1)} %param.8) | copy-start | bytes 3076
  22.3 10.6 %copy-start.1 = (bf16[128,512]{1,0:T(8,128)(2,1)S(1)}, bf16[128,512]{1,0:T(8,128)(2,1)}, u32[]{:S(2)}) copy-start(bf16[128,512]{1,0:T(8,128)(2,1)} %param.7) | copy-start | bytes 393220
  22.3 113.6 %all-to-all-start.1 = ((bf16[16,256,512]{2,1,0:T(8,128)(2,1)}), bf16[16,256,512]{2,1,0:T(8,128)(2,1)}, u32[]{:S(2)}, u32[]{:S(2)}) async-start(bf16[16,256,512]{2,1,0:T(8,128)(2,1)} %stack.2), calls=%async_computation.2 | async-start | bytes 8388608 | tf_op jit(solution)/shard_map/all_to_all | solution.py:56
  32.8 128.0 %reduce-scatter.3.cloned.1.call-start = ((), (), s32[]{:S(2)}) async-start(), calls=%async_computation.8 | async-start | bytes 4456448 | tf_op jit(solution)/shard_map/reduce_scatter | solution.py:64
  39.6 114.9 %copy-start.3 = (s32[2]{0:T(128)S(1)}, s32[2]{0:T(128)}, u32[]{:S(2)}) copy-start(s32[2]{0:T(128)} %param.12) | copy-start | bytes 28
  139.5 20.4 %all-to-all-start.2 = ((f32[16,8,512]{2,1,0:T(8,128)}), f32[16,8,512]{2,1,0:T(8,128)S(1)}, u32[]{:S(2)}, u32[]{:S(2)}) async-start(f32[16,8,512]{2,1,0:T(8,128)} %fusion.10), calls=%async_computation.3 | async-start | bytes 524288 | tf_op jit(solution)/shard_map/all_to_all | solution.py:71
  154.5 159.1 %reduce-scatter.5.cloned.1.call-start = ((), (), s32[]{:S(2)}) async-start(), calls=%async_computation.9 | async-start | bytes 8912896 | tf_op jit(solution)/shard_map/reduce_scatter | solution.py:92
  178.2 10.6 %all-to-all-start.3 = ((f32[16,4,8]{2,1,0:T(4,128)}), f32[16,4,8]{2,1,0:T(4,128)S(1)}, u32[]{:S(2)}, u32[]{:S(2)}) async-start(f32[16,4,8]{2,1,0:T(4,128)} %broadcast_in_dim.8), calls=%async_computation.4 | async-start | bytes 65536 | tf_op jit(solution)/shard_map/all_to_all | solution.py:15
  188.8 74.0 %all-to-all-start.5 = ((f32[16,128,256]{2,1,0:T(8,128)}), f32[16,128,256]{2,1,0:T(8,128)S(1)}, u32[]{:S(2)}, u32[]{:S(2)}) async-start(f32[16,128,256]{2,1,0:T(8,128)} %convolution_bitcast_fusion.1), calls=%async_computation.6 | async-start | bytes 4194304 | tf_op jit(solution)/shard_map/all_to_all | solution.py:41
Sparse Core Ops, SparseCore 0:
  39.7 111.4 reduce-scatter.2
  177.7 135.8 reduce-scatter.4
